TPU v7x, 512 devices: a whole 4x8x8 slice. The times are simulated.
512 devices in a mesh: subset: 8 (over x, z_lo), tile: 64 (over y, z_hi, core).
Axes of the slice: x: 4, y: 8, z: 8 (z_hi: 4, z_lo: 2; z = z_hi * 2 + z_lo), core: 2. Of those that a mesh axis runs over, the one named last changes fastest.
Arguments:
- images: float32 [256, 131072], P('subset', 'tile'), may hold values from 0.5 to 2
- system_tiles: bfloat16 [8, 2048, 128, 128], P('subset', 'tile'), may hold values from 5.197525e-05 to 0.0025939941
- tile_vox: int32 [8, 2048], P('subset', 'tile'), may hold values from 0 to 15, as said below
- tile_ray: int32 [8, 2048], P('subset', 'tile'), may hold values from 0 to 63, as said below
- live_blocks: int32 [8, 64], P('subset', 'tile'), may hold values from 1 to 1, as said below
- counts: int32 [8, 256, 8192], P('subset', None, 'tile'), may hold values from 1 to 7
Outputs:
- updated: float32 [256, 131072], P('subset', 'tile')
Inputs may be any that keep to these rules, and one draw needn't show every extreme that they name: `tile_vox`: within each image tile and subset, the first 16 tile slots name every voxel block of that image tile once. `tile_ray`: in each subset every ray block is named by one of the first 1 tile slots of some image tile. `live_blocks`: slots in use are the first ones of an image tile; in every draw some image tile uses all of its blocks.
All inputs are finite; a program needn't handle non-finite values.
Results may differ from a plain program's by a relative error of at most 0.00063.
Values may be sent and summed in bfloat16 or wider, within the bound.
A program may use at most 64 MiB of HBM per device.

v0:
```python
import jax
import jax.numpy as jnp
from jax import lax
from jax.sharding import PartitionSpec as P

TILE_GROUP = 32
ROUNDS = 4


HIGHEST = lax.Precision.HIGHEST


def shifted(array, axis, by):
    peers = lax.axis_size(axis)
    return lax.ppermute(array, axis, [(i, (i + by) % peers) for i in range(peers)])


def project(panel, system_tiles, voxel_index, ray_index, live_count, ray_total):
    frame_count = panel.shape[0]
    block_size = system_tiles.shape[-1]
    lowered = panel.astype(jnp.bfloat16).reshape(frame_count, -1, block_size)
    ray_ids = jnp.arange(ray_total, dtype=jnp.int32)

    def project_accumulate(counter, running):
        chosen = jnp.take(lowered, voxel_index, axis=1)
        contrib = jnp.einsum(
            "ftv,trv->tfr", chosen, system_tiles, preferred_element_type=jnp.float32
        )
        onehot = (ray_index[None, :] == ray_ids[:, None]).astype(jnp.float32)
        return running + jnp.einsum("bt,tfr->fbr", onehot, contrib, precision=HIGHEST)

    start_value = jnp.zeros((frame_count, ray_total, block_size), jnp.float32)
    summed = lax.fori_loop(0, live_count, project_accumulate, start_value)
    return summed.reshape(frame_count, ray_total * block_size)


def backproject(all_ratios, system_tiles, voxel_index, ray_index, live_count, vox_blocks):
    frame_count = all_ratios.shape[0]
    block_size = system_tiles.shape[-1]
    ratio_grid = all_ratios.reshape(frame_count, -1, block_size)
    vox_ids = jnp.arange(vox_blocks, dtype=jnp.int32)

    def backproject_accumulate(counter, running):
        chosen = jnp.take(ratio_grid, ray_index, axis=1)
        contrib = jnp.einsum(
            "ftr,trv->tfv", chosen, system_tiles, preferred_element_type=jnp.float32
        )
        onehot = (voxel_index[None, :] == vox_ids[:, None]).astype(jnp.float32)
        return running + jnp.einsum("ct,tfv->fcv", onehot, contrib, precision=HIGHEST)

    start_value = jnp.zeros((frame_count, vox_blocks, block_size), jnp.float32)
    return lax.fori_loop(0, live_count, backproject_accumulate, start_value)


def shards(images, system_tiles, tile_vox, tile_ray, live_blocks, counts):
    frame_count = images.shape[0]
    block_size = system_tiles.shape[-1]
    vox_blocks = images.shape[1] // block_size
    tile_set = system_tiles[0]
    voxel_index = tile_vox[0]
    ray_index = tile_ray[0]
    live_count = live_blocks[0, 0]
    measured = counts[0]
    ray_total = measured.shape[1] // block_size * lax.axis_size("tile")
    slot_count = tile_set.shape[0]
    tile_mask = (jnp.arange(slot_count, dtype=jnp.int32) // TILE_GROUP < live_count).astype(
        jnp.float32
    )
    column = jnp.einsum(
        "r,trv->tv",
        jnp.ones((block_size,), jnp.bfloat16),
        tile_set,
        preferred_element_type=jnp.float32,
    )
    vox_onehot = (voxel_index[None, :] == jnp.arange(vox_blocks, dtype=jnp.int32)[:, None]).astype(
        jnp.float32
    )
    sensitivity = jnp.einsum(
        "ct,tv->cv", vox_onehot, column * tile_mask[:, None], precision=HIGHEST
    )
    position = lax.axis_index("subset")
    subset_count = lax.axis_size("subset")
    panel = images
    for round_index in range(ROUNDS):
        panel_index = (position - round_index) % subset_count
        counts_now = lax.dynamic_slice_in_dim(measured, panel_index * frame_count, frame_count, 0)
        counts_now = counts_now.astype(jnp.float32)
        partial_value = project(panel, tile_set, voxel_index, ray_index, live_count, ray_total)
        own_sums = lax.psum_scatter(partial_value, "tile", scatter_dimension=1, tiled=True)
        ratios = (counts_now / own_sums).astype(jnp.bfloat16)
        all_ratios = lax.all_gather(ratios, "tile", axis=1, tiled=True)
        back_sum = backproject(all_ratios, tile_set, voxel_index, ray_index, live_count, vox_blocks)
        shaped = panel.reshape(frame_count, vox_blocks, block_size)
        panel = (shaped * back_sum / sensitivity[None]).reshape(
            frame_count, vox_blocks * block_size
        )
        if round_index + 1 < ROUNDS:
            panel = shifted(panel, "subset", 1)
    return panel


def solution(mesh):
    in_specs = (
        P("subset", "tile"),
        P("subset", "tile", None, None),
        P("subset", "tile"),
        P("subset", "tile"),
        P("subset", "tile"),
        P("subset", None, "tile"),
    )
    out_specs = P("subset", "tile")
    return jax.shard_map(shards, mesh=mesh, in_specs=in_specs, out_specs=out_specs, check_vma=False)
```

profile of v0, /device:TPU:1, one launch (start us, length us, event | category | flops | bytes accessed | tf_op | source)
XLA Modules:
  0.0 1004.2 jit_solution(4518618025597076370)
XLA Ops:
  11.3 1.6 while.104
  12.9 1.6 copy.79
  16.1 150.0 %reduce-scatter.5.cloned.1.call-done = f32[32,128]{1,0:T(8,128)} async-done(((f32[32,8192]{1,0:T(8,128)}), f32[32,128]{1,0:T(8,128)}) %reduce-scatter.5.cloned.1.call-update) | async-done | bytes 16400 | tf_op jit(solution)/shard_map/reduce_scatter | solution.py:89
  166.8 85.9 %all_gather.12 = bf16[32,8192]{1,0:T(8,128)(2,1)S(1)} all-gather(bf16[32,128]{1,0:T(8,128)(2,1)S(1)} %fusion.73), channel_id=1, replica_groups=mesh['subset'=8,'tile'=64] {'tile'}, dimensions={1}, use_global_device_ids=true | all-gather | bytes 532480 | tf_op jit(solution)/shard_map/all_gather | solution.py:91
  256.0 2.4 collective-permute-start
  258.4 9.3 collective-permute-done
  270.1 1.6 while.106
  271.7 1.6 copy.78
  273.5 139.1 %reduce-scatter.7.cloned.1.call-done = f32[32,128]{1,0:T(8,128)} async-done(((f32[32,8192]{1,0:T(8,128)}), f32[32,128]{1,0:T(8,128)}) %reduce-scatter.7.cloned.1.call-update) | async-done | bytes 16400 | tf_op jit(solution)/shard_map/reduce_scatter | solution.py:89
  413.4 85.9 %all_gather.13 = bf16[32,8192]{1,0:T(8,128)(2,1)S(1)} all-gather(bf16[32,128]{1,0:T(8,128)(2,1)S(1)} %fusion.72), channel_id=1, replica_groups=mesh['subset'=8,'tile'=64] {'tile'}, dimensions={1}, use_global_device_ids=true | all-gather | bytes 532480 | tf_op jit(solution)/shard_map/all_gather | solution.py:91
  501.2 1.4 while.107
  502.8 2.5 collective-permute-start.1
  505.2 9.2 collective-permute-done.1
  517.0 1.8 while.108
  518.8 1.6 copy.77
  520.6 139.3 %reduce-scatter.9.cloned.1.call-done = f32[32,128]{1,0:T(8,128)} async-done(((f32[32,8192]{1,0:T(8,128)}), f32[32,128]{1,0:T(8,128)}) %reduce-scatter.9.cloned.1.call-update) | async-done | bytes 16400 | tf_op jit(solution)/shard_map/reduce_scatter | solution.py:89
  660.6 85.9 %all_gather.14 = bf16[32,8192]{1,0:T(8,128)(2,1)S(1)} all-gather(bf16[32,128]{1,0:T(8,128)(2,1)S(1)} %fusion.71), channel_id=1, replica_groups=mesh['subset'=8,'tile'=64] {'tile'}, dimensions={1}, use_global_device_ids=true | all-gather | bytes 532480 | tf_op jit(solution)/shard_map/all_gather | solution.py:91
  748.4 1.4 while.109
  750.0 2.4 collective-permute-start.2
  752.4 9.3 collective-permute-done.2
  764.2 1.6 while.110
  765.8 1.6 copy.76
  767.5 139.3 %reduce-scatter.11.cloned.1.call-done = f32[32,128]{1,0:T(8,128)} async-done(((f32[32,8192]{1,0:T(8,128)}), f32[32,128]{1,0:T(8,128)}) %reduce-scatter.11.cloned.1.call-update) | async-done | bytes 16400 | tf_op jit(solution)/shard_map/reduce_scatter | solution.py:89
  907.6 86.0 %all_gather.15 = bf16[32,8192]{1,0:T(8,128)(2,1)S(1)} all-gather(bf16[32,128]{1,0:T(8,128)(2,1)S(1)} %fusion.70), channel_id=1, replica_groups=mesh['subset'=8,'tile'=64] {'tile'}, dimensions={1}, use_global_device_ids=true | all-gather | bytes 532480 | tf_op jit(solution)/shard_map/all_gather | solution.py:91
  (110 shorter events, 28.8 us)
Async XLA Ops:
  6.5 3.0 copy-start
  6.5 159.5 %reduce-scatter.5.cloned.1.call-start = ((), (), s32[]{:S(2)}) async-start(), calls=%async_computation.4 | async-start | bytes 1064960 | tf_op jit(solution)/shard_map/reduce_scatter | solution.py:89
  6.5 0.7 copy-start.4
  7.3 0.7 copy-start.3
  8.0 245.5 %copy-start.5 = (pred[32]{0:T(512)(128)(4,1)}, pred[32]{0:T(512)(128)(4,1)S(1)}, u32[]{:S(2)}) copy-start(pred[32]{0:T(512)(128)(4,1)S(1)} %get-tuple-element.935) | copy-start | bytes 100
  8.0 260.4 %copy-start.9 = (pred[32]{0:T(512)(128)(4,1)}, pred[32]{0:T(512)(128)(4,1)S(1)}, u32[]{:S(2)}) copy-start(pred[32]{0:T(512)(128)(4,1)S(1)} %get-tuple-element.936) | copy-start | bytes 100
  8.0 259.8 %copy-start.13 = (s32[1024]{0:T(1024)}, s32[1024]{0:T(1024)S(1)}, u32[]{:S(2)}) copy-start(s32[1024]{0:T(1024)S(1)} %pad_clamp_fusion.1) | copy-start | bytes 12292
  14.6 0.9 copy-start.1
  14.6 398.1 %reduce-scatter.7.cloned.1.call-start = ((), (), s32[]{:S(2)}) async-start(), calls=%async_computation.5 | async-start | bytes 1064960 | tf_op jit(solution)/shard_map/reduce_scatter | solution.py:89
  15.6 237.2 %copy-start.12 = (s32[1024]{0:T(1024)}, s32[1024]{0:T(1024)S(1)}, u32[]{:S(2)}) copy-start(s32[1024]{0:T(1024)S(1)} %pad_clamp_fusion) | copy-start | bytes 12292
  15.6 150.4 %copy-start.2 = (s32[1,256,128]{2,1,0:T(8,128)S(1)}, s32[1,256,128]{2,1,0:T(8,128)}, u32[]{:S(2)}) copy-start(s32[1,256,128]{2,1,0:T(8,128)} %param.31) | copy-start | bytes 393220
  256.0 11.7 %collective-permute-start = (f32[32,2048]{1,0:T(8,128)S(1)}, f32[32,2048]{1,0:T(8,128)S(1)}, u32[]{:S(2)}, u32[]{:S(2)}) collective-permute-start(f32[32,2048]{1,0:T(8,128)S(1)} %bitcast.224), channel_id=1, source_target_pairs={{0,64},{64,128},{128,192},{192,256},{256,320},{320,384},{384,448},... | collective-permute-start | bytes 786440 | tf_op jit(solution)/shard_map/ppermute | solution.py:15
  273.4 386.5 %reduce-scatter.9.cloned.1.call-start = ((), (), s32[]{:S(2)}) async-start(), calls=%async_computation.6 | async-start | bytes 1064960 | tf_op jit(solution)/shard_map/reduce_scatter | solution.py:89
  499.4 0.7 copy-start.6
  502.8 11.7 %collective-permute-start.1 = (f32[32,2048]{1,0:T(8,128)S(1)}, f32[32,2048]{1,0:T(8,128)S(1)}, u32[]{:S(2)}, u32[]{:S(2)}) collective-permute-start(f32[32,2048]{1,0:T(8,128)S(1)} %bitcast.225), channel_id=1, source_target_pairs={{0,64},{64,128},{128,192},{192,256},{256,320},{320,384},{384,448},... | collective-permute-start | bytes 786440 | tf_op jit(solution)/shard_map/ppermute | solution.py:15
  514.5 0.7 copy-start.10
  520.4 386.4 %reduce-scatter.11.cloned.1.call-start = ((), (), s32[]{:S(2)}) async-start(), calls=%async_computation.7 | async-start | bytes 1064960 | tf_op jit(solution)/shard_map/reduce_scatter | solution.py:89
  746.6 0.7 copy-start.7
  750.0 11.7 %collective-permute-start.2 = (f32[32,2048]{1,0:T(8,128)S(1)}, f32[32,2048]{1,0:T(8,128)S(1)}, u32[]{:S(2)}, u32[]{:S(2)}) collective-permute-start(f32[32,2048]{1,0:T(8,128)S(1)} %bitcast.226), channel_id=1, source_target_pairs={{0,64},{64,128},{128,192},{192,256},{256,320},{320,384},{384,448},... | collective-permute-start | bytes 786440 | tf_op jit(solution)/shard_map/ppermute | solution.py:15
  761.7 0.7 copy-start.11
  993.6 0.7 copy-start.8
Sparse Core Ops, SparseCore 0:
  14.7 151.2 reduce-scatter.4
  273.5 139.1 reduce-scatter.6
  520.6 139.3 reduce-scatter.8
  767.6 139.2 reduce-scatter.10
where the time goes:
time: 1010 us; the launch traced here: 1000 us
  waiting for transfers between devices  596 us (59%)
  blocking collectives  344 us (34%)
  local copies, waits for them, and re-layouts  15.7 us (2%)
  between operations  14.4 us (1%)
  matrix products  11.2 us (1%)
  loops' own time  10.7 us (1%)
    reduce_scatter x4, waiting for transfers between devices, shards(): lax.psum_scatter(partial_value, 'tile', scatter_dimension=1, tiled=True)  568 us
    all_gather x4, blocking collectives, shards(): all_ratios = lax.all_gather(ratios, 'tile', axis=1, tiled=True)  344 us
    ppermute x3, waiting for transfers between devices, shifted(): lax.ppermute(array, axis, [(i, (i + by) % peers) for i in range(peers)])  27.8 us
  transfers between devices with their start and end apart: 7, of which 7 were waited for; matrix products, arithmetic and copies ran while one was open for 0% of the time, Pallas kernels for 0%

commit v1 on v0

v1 whole, which is shorter than its diff:
```python
import functools

import jax
import jax.numpy as jnp
from jax import lax
from jax.experimental import pallas as pl
from jax.experimental.pallas import tpu as pltpu
from jax.sharding import PartitionSpec as P

TILE_GROUP = 32
ROUNDS = 4
SUBSETS = 8
SLOTS = 32
VOX = 16
RAYS = 64
B = 128
NY = 8
NZ = 4
FP = 32
HALVES = 2
F = FP // HALVES
OWN = RAYS // 2

PREV_R, PREV_V, VOX_OF, RATIO_OF, LAST_R, LAST_V, TABLE = 0, 32, 64, 96, 128, 192, 256

f32 = jnp.float32
bf16 = jnp.bfloat16


def prepare(vox_ref, ray_ref, live_ref, table_ref):
    core = lax.rem(lax.axis_index("tile"), 2)
    live = live_ref[0, 0]
    for i in range(TABLE):
        table_ref[i] = SLOTS
    for t in range(SLOTS):
        vox, ray = vox_ref[0, t], ray_ref[0, t]
        table_ref[VOX_OF + t] = vox
        table_ref[RATIO_OF + t] = jnp.where(lax.rem(ray, 2) == core, 0, OWN) + lax.div(ray, 2)
        alive = t // TILE_GROUP < live
        for last, prev, block in ((LAST_R, PREV_R, ray), (LAST_V, PREV_V, vox)):
            before = table_ref[last + block]
            table_ref[prev + t] = before
            table_ref[last + block] = jnp.where(alive, t, before)


def fused(
    table, images, tiles, counts, out,
    low_0a, low_0b, low_1a, low_1b, low_2a, low_2b, low_3a, low_3b,
    rest, send_high, send_low, acc_a, acc_b, acc_back, inverse,
    send_c, recv_c, send_y, recv_y, send_z, recv_z, ratio_a, ratio_b, cnt,
    s_c, r_c, s_y, r_y, s_z, r_z, s_g, r_g, s_p, r_p, s_h, r_h, s_l, r_l, s_n, r_n,
):
    low = ((low_0a, low_0b), (low_1a, low_1b), (low_2a, low_2b), (low_3a, low_3b))
    acc = (acc_a, acc_b)
    ratio = (ratio_a, ratio_b)
    subset = lax.axis_index("subset")
    tile = lax.axis_index("tile")
    core = lax.rem(tile, 2)
    z = lax.rem(lax.div(tile, 2), NZ)
    y = lax.div(tile, 2 * NZ)

    def at(y_of, z_of, c_of):
        return {"tile": (y_of * NZ + z_of) * 2 + c_of}

    partner = at(y, z, 1 - core)
    y_of = [None] + [lax.rem(y + k, NY) for k in range(1, NY)]
    y_peers = [None] + [at(y_of[k], z, core) for k in range(1, NY)]
    z_peers = [None] + [at(y, lax.rem(z + k, NZ), core) for k in range(1, NZ)]
    ahead = {"subset": lax.rem(subset + 1, SUBSETS)}
    behind = {"subset": lax.rem(subset + SUBSETS - 1, SUBSETS)}
    everyone = [partner] + y_peers[1:] + z_peers[1:] + [ahead, behind]
    far_first_y = (4, 3, 5, 2, 6, 1, 7)
    far_first_z = (2, 1, 3)

    barrier = pltpu.get_barrier_semaphore()
    for peer in everyone:
        pl.semaphore_signal(barrier, inc=1, device_id=peer, device_id_type=pl.DeviceIdType.MESH)

    def remote(src, dst, send, recv, peer):
        return pltpu.make_async_remote_copy(
            src_ref=src, dst_ref=dst, send_sem=send, recv_sem=recv,
            device_id=peer, device_id_type=pl.DeviceIdType.MESH,
        )

    def await_bytes(ref, sem):
        pltpu.make_async_copy(ref, ref, sem).wait()

    def frames(h):
        return slice(h * F, (h + 1) * F)

    for h in range(HALVES):
        acc[h][SLOTS] = jnp.zeros((F, B), f32)
        for v in range(VOX):
            low[0][h][v] = images[frames(h), v * B : (v + 1) * B].astype(bf16)
    acc_back[SLOTS] = jnp.zeros((F, B), f32)
    for r in range(ROUNDS):
        panel = lax.rem(subset - r + SUBSETS, SUBSETS)
        rows = pl.ds(pl.multiple_of(panel * FP, FP), FP)
        cnt[z, r] = counts[0, rows, :].astype(f32).astype(bf16)

    def project(r, h):
        for t in range(SLOTS):
            chosen = low[r][h][table[VOX_OF + t]]
            product = lax.dot_general(
                chosen, tiles[0, t], (((1,), (1,)), ((), ())), preferred_element_type=f32
            )
            acc[h][t] = product + acc[h][table[PREV_R + t]]
        for j in range(OWN):
            send_c[h, j] = acc[h][table[LAST_R + 2 * j + 1 - core]].astype(bf16)

    def backproject(h):
        for t in range(SLOTS):
            product = jnp.dot(
                ratio[h][table[RATIO_OF + t]], tiles[0, t], preferred_element_type=f32
            )
            acc_back[t] = product + acc_back[table[PREV_V + t]]

    for r in range(ROUNDS):
        p = r % 2
        last = r + 1 == ROUNDS
        for h in range(HALVES):
            if r > 0:
                await_bytes(low[r][h], r_h.at[r - 1, h])
                await_bytes(send_c.at[h], s_c.at[h])
            project(r, h)
            if r == 0 and h == 0:
                pl.semaphore_wait(barrier, len(everyone))
                for k in far_first_z:
                    remote(cnt.at[z], cnt.at[z], s_n, r_n, z_peers[k]).start()
            remote(send_c.at[h], recv_c.at[h], s_c.at[h], r_c.at[h], partner).start()
        for h in range(HALVES):
            await_bytes(recv_c.at[h], r_c.at[h])
            if r > 0:
                await_bytes(recv_y.at[h], s_y.at[h])
                await_bytes(ratio[h].at[pl.ds(0, OWN)], s_p.at[h])
            for j in range(OWN):
                own = acc[h][table[LAST_R + 2 * j + core]]
                send_y[h, j] = (own + recv_c[h, j].astype(f32)).astype(bf16)
            for k in far_first_y:
                remote(
                    send_y.at[h, pl.ds(y_of[k] * NZ, NZ)], recv_y.at[h, k - 1],
                    s_y.at[h], r_y.at[h], y_peers[k],
                ).start()
        if r == 0:
            ones = jnp.ones((F, B), bf16)
            for t in range(SLOTS):
                column = jnp.dot(ones, tiles[0, t], preferred_element_type=f32)
                acc_back[t] = column + acc_back[table[PREV_V + t]]
            for v in range(VOX):
                inverse[v] = 1.0 / acc_back[table[LAST_V + v]]
            await_bytes(cnt.at[pl.ds(0, NZ - 1)], r_n)
        for h in range(HALVES):
            await_bytes(recv_y.at[h], r_y.at[h])
            if r > 1:
                await_bytes(recv_z.at[p, h], s_z.at[p, h])
            for b in range(NZ):
                total = send_y[h, y * NZ + b].astype(f32)
                for k in range(NY - 1):
                    total = total + recv_y[h, k, b].astype(f32)
                send_z[p, h, b] = total.astype(bf16)
            for k in far_first_z:
                remote(
                    send_z.at[p, h], recv_z.at[p, h, k - 1], s_z.at[p, h], r_z.at[p, h], z_peers[k]
                ).start()
        for h in range(HALVES):
            await_bytes(recv_z.at[p, h], r_z.at[p, h])
            if r > 0:
                await_bytes(ratio[h].at[pl.ds(0, NZ * (NY - 1))], s_g.at[h])
            for b in range(NZ):
                even = send_z[p, h, b].astype(f32) + recv_z[p, h, 1, b].astype(f32)
                odd = recv_z[p, h, 0, b].astype(f32) + recv_z[p, h, 2, b].astype(f32)
                measured = cnt[b, r, frames(h), :].astype(f32)
                ratio[h][y * NZ + b] = (measured / (even + odd)).astype(bf16)
            mine = ratio[h].at[pl.ds(y * NZ, NZ)]
            for k in far_first_y:
                remote(mine, mine, s_g.at[h], r_g.at[h], y_peers[k]).start()
        for h in range(HALVES):
            await_bytes(ratio[h].at[pl.ds(0, NZ * (NY - 1))], r_g.at[h])
            remote(
                ratio[h].at[pl.ds(0, OWN)], ratio[h].at[pl.ds(OWN, OWN)], s_p.at[h], r_p.at[h], partner
            ).start()
        for h in range(HALVES):
            await_bytes(ratio[h].at[pl.ds(OWN, OWN)], r_p.at[h])
            backproject(h)
            if r > 0:
                await_bytes(rest.at[r - 1, h], r_l.at[r - 1, h])
                if not last:
                    await_bytes(send_high.at[h], s_h.at[r - 1, h])
                    await_bytes(send_low.at[h], s_l.at[r - 1, h])
            for v in range(VOX):
                if r == 0:
                    held = images[frames(h), v * B : (v + 1) * B]
                else:
                    held = low[r][h][v].astype(f32) + rest[r - 1, h, v].astype(f32)
                held = held * acc_back[table[LAST_V + v]] * inverse[v]
                if last:
                    out[frames(h), v * B : (v + 1) * B] = held
                else:
                    high = held.astype(bf16)
                    send_high[h, v] = high
                    send_low[h, v] = (held - high.astype(f32)).astype(bf16)
            if not last:
                remote(send_high.at[h], low[r + 1][h], s_h.at[r, h], r_h.at[r, h], ahead).start()
                remote(send_low.at[h], rest.at[r, h], s_l.at[r, h], r_l.at[r, h], ahead).start()

    await_bytes(cnt.at[pl.ds(0, NZ - 1)], s_n)
    for h in range(HALVES):
        await_bytes(send_c.at[h], s_c.at[h])
        await_bytes(recv_y.at[h], s_y.at[h])
        for p in range(2):
            await_bytes(recv_z.at[p, h], s_z.at[p, h])
        await_bytes(ratio[h].at[pl.ds(0, NZ * (NY - 1))], s_g.at[h])
        await_bytes(ratio[h].at[pl.ds(0, OWN)], s_p.at[h])
        await_bytes(send_high.at[h], s_h.at[ROUNDS - 2, h])
        await_bytes(send_low.at[h], s_l.at[ROUNDS - 2, h])


def shards(images, system_tiles, tile_vox, tile_ray, live_blocks, counts):
    smem = pl.BlockSpec(memory_space=pltpu.SMEM)
    vmem = pl.BlockSpec(memory_space=pltpu.VMEM)
    table = pl.pallas_call(
        prepare,
        out_shape=jax.ShapeDtypeStruct((TABLE,), jnp.int32),
        in_specs=[smem] * 3,
        out_specs=smem,
        name="prepare",
    )(tile_vox, tile_ray, live_blocks)
    half = pltpu.VMEM((VOX, F, B), bf16)
    dma = pltpu.SemaphoreType.DMA
    return pl.pallas_call(
        fused,
        out_shape=jax.ShapeDtypeStruct(images.shape, f32),
        in_specs=[smem, vmem, vmem, vmem],
        out_specs=vmem,
        scratch_shapes=[half] * (2 * ROUNDS)
        + [
            pltpu.VMEM((ROUNDS - 1, HALVES, VOX, F, B), bf16),
            pltpu.VMEM((HALVES, VOX, F, B), bf16),
            pltpu.VMEM((HALVES, VOX, F, B), bf16),
            pltpu.VMEM((SLOTS + 1, F, B), f32),
            pltpu.VMEM((SLOTS + 1, F, B), f32),
            pltpu.VMEM((SLOTS + 1, F, B), f32),
            pltpu.VMEM((VOX, F, B), f32),
            pltpu.VMEM((HALVES, OWN, F, B), bf16),
            pltpu.VMEM((HALVES, OWN, F, B), bf16),
            pltpu.VMEM((HALVES, OWN, F, B), bf16),
            pltpu.VMEM((HALVES, NY - 1, NZ, F, B), bf16),
            pltpu.VMEM((2, HALVES, NZ, F, B), bf16),
            pltpu.VMEM((2, HALVES, NZ - 1, NZ, F, B), bf16),
            pltpu.VMEM((RAYS, F, B), bf16),
            pltpu.VMEM((RAYS, F, B), bf16),
            pltpu.VMEM((NZ, ROUNDS, FP, B), bf16),
            dma((HALVES,)), dma((HALVES,)),
            dma((HALVES,)), dma((HALVES,)),
            dma((2, HALVES)), dma((2, HALVES)),
            dma((HALVES,)), dma((HALVES,)),
            dma((HALVES,)), dma((HALVES,)),
            dma((ROUNDS - 1, HALVES)), dma((ROUNDS - 1, HALVES)),
            dma((ROUNDS - 1, HALVES)), dma((ROUNDS - 1, HALVES)),
            dma, dma,
        ],
        compiler_params=pltpu.CompilerParams(collective_id=0, has_side_effects=True),
        name="fused",
    )(table, images, system_tiles, counts)


def solution(mesh):
    in_specs = (
        P("subset", "tile"),
        P("subset", "tile", None, None),
        P("subset", "tile"),
        P("subset", "tile"),
        P("subset", "tile"),
        P("subset", None, "tile"),
    )
    out_specs = P("subset", "tile")
    return jax.shard_map(shards, mesh=mesh, in_specs=in_specs, out_specs=out_specs, check_vma=False)
```

time: 1010 us -> 120 us (0.12)
  waiting for transfers between devices: 596 us -> 0 us
  blocking collectives: 344 us -> 0 us
  Pallas kernels: 0 us -> 118 us
  local copies, waits for them, and re-layouts: 15.7 us -> 1.67 us
  between operations: 14.4 us -> 0.67 us
  matrix products: 11.2 us -> 0 us
  loops' own time: 10.7 us -> 0 us
    reduce_scatter x4 -> x0, waiting for transfers between devices: 568 us -> none  [shards(): lax.psum_scatter(partial_value, 'tile', scatter_dimension=1, tiled=True)]
    all_gather x4 -> x0, blocking collectives: 344 us -> none  [shards(): all_ratios = lax.all_gather(ratios, 'tile', axis=1, tiled=True)]
    pallas_call x0 -> x2, Pallas kernels: none -> 118 us  [the longest x1 116 us: shards(): pl.pallas_call(fused, out_shape=jax.ShapeDtypeStruct(images.shape, f32),...]
    ppermute x3 -> x0, waiting for transfers between devices: 27.8 us -> none  [shifted(): lax.ppermute(array, axis, [(i, (i + by) % peers) for i in range(peers)])]
    dot_general x18 -> x0, matrix products: 11.2 us -> none  [the longest x4 3.79 us: project_accumulate(): jnp.einsum('bt,tfr->fbr', onehot, contrib, precision=HIGHEST)]
    another operation x8 -> x0, loops' own time: 10.7 us -> none  [the longest x4 5.46 us: project(): summed = lax.fori_loop(0, live_count, project_accumulate, start_value)]
  transfers between devices with their start and end apart: 7 -> 0, of which waited for: 7 -> 0; matrix products, arithmetic and copies ran while one was open for 0% -> 0% of each run, Pallas kernels for 0% -> 0%
where the time goes in v1:
time: 120 us
  Pallas kernels  118 us (98%)
  local copies, waits for them, and re-layouts  1.67 us (1%)
    pallas_call x1, Pallas kernels, shards(): pl.pallas_call(fused, out_shape=jax.ShapeDtypeStruct(images.shape, f32),...  116 us

profile of v1, /device:TPU:1, one launch (start us, length us, event | category | flops | bytes accessed | tf_op | source)
XLA Modules:
  0.0 120.2 jit_solution(3689786519152410852)
XLA Ops:
  0.7 1.7 %prepare.1.table = s32[256]{0:T(256)} custom-call(s32[1,32]{1,0:T(1,128)} %vox_ref.1, s32[1,32]{1,0:T(1,128)} %ray_ref.1, s32[1,1]{1,0:T(1,128)S(6)} %copy.8.live_ref), custom_call_target="tpu_custom_call" | custom-call | tf_op jit(solution)/shard_map/prepare/pallas_call | solution.py:221
  2.3 116.2 %fused.1 = f32[32,2048]{1,0:T(8,128)} custom-call(s32[256]{0:T(256)} %prepare.1.table, f32[32,2048]{1,0:T(8,128)} %images.1, bf16[1,32,128,128]{3,2,1,0:T(8,128)(2,1)} %tiles.1, s32[1,256,128]{2,1,0:T(8,128)} %counts.1), custom_call_target="tpu_custom_call" | custom-call | tf_op jit(solution)/shard_map/fused/pallas_call | solution.py:230
  118.6 1.7 %copy.9 = f32[32,2048]{1,0:T(8,128)} copy(f32[32,2048]{1,0:T(8,128)} %fused.1) | data formatting | bytes 524288

commit v2 on v1

--- a/solution.py
+++ b/solution.py
@@ -115,93 +115,118 @@
             )
             acc_back[t] = product + acc_back[table[PREV_V + t]]
 
+    def stage_c(r, h):
+        if r > 0:
+            await_bytes(low[r][h], r_h.at[r - 1, h])
+            await_bytes(send_c.at[h], s_c.at[h])
+        project(r, h)
+        if r == 0 and h == 0:
+            pl.semaphore_wait(barrier, len(everyone))
+        remote(send_c.at[h], recv_c.at[h], s_c.at[h], r_c.at[h], partner).start()
+
+    def stage_y(r, h):
+        await_bytes(recv_c.at[h], r_c.at[h])
+        if r > 0:
+            await_bytes(recv_y.at[h], s_y.at[h])
+            await_bytes(ratio[h].at[pl.ds(0, OWN)], s_p.at[h])
+        for j in range(OWN):
+            own = acc[h][table[LAST_R + 2 * j + core]]
+            send_y[h, j] = (own + recv_c[h, j].astype(f32)).astype(bf16)
+        for k in far_first_y:
+            remote(
+                send_y.at[h, pl.ds(y_of[k] * NZ, NZ)], recv_y.at[h, k - 1],
+                s_y.at[h], r_y.at[h], y_peers[k],
+            ).start()
+
+    def stage_z(r, h):
+        p = r % 2
+        await_bytes(recv_y.at[h], r_y.at[h])
+        if r > 1:
+            await_bytes(recv_z.at[p, h], s_z.at[p, h])
+        for b in range(NZ):
+            total = send_y[h, y * NZ + b].astype(f32)
+            for k in range(NY - 1):
+                total = total + recv_y[h, k, b].astype(f32)
+            send_z[p, h, b] = total.astype(bf16)
+        for k in far_first_z:
+            remote(
+                send_z.at[p, h], recv_z.at[p, h, k - 1], s_z.at[p, h], r_z.at[p, h], z_peers[k]
+            ).start()
+
+    def stage_g(r, h):
+        p = r % 2
+        await_bytes(recv_z.at[p, h], r_z.at[p, h])
+        if r > 0:
+            await_bytes(ratio[h].at[pl.ds(0, NZ * (NY - 1))], s_g.at[h])
+        for b in range(NZ):
+            even = send_z[p, h, b].astype(f32) + recv_z[p, h, 1, b].astype(f32)
+            odd = recv_z[p, h, 0, b].astype(f32) + recv_z[p, h, 2, b].astype(f32)
+            measured = cnt[b, r, frames(h), :].astype(f32)
+            ratio[h][y * NZ + b] = (measured / (even + odd)).astype(bf16)
+        mine = ratio[h].at[pl.ds(y * NZ, NZ)]
+        for k in far_first_y:
+            remote(mine, mine, s_g.at[h], r_g.at[h], y_peers[k]).start()
+
+    def stage_p(h):
+        await_bytes(ratio[h].at[pl.ds(0, NZ * (NY - 1))], r_g.at[h])
+        remote(
+            ratio[h].at[pl.ds(0, OWN)], ratio[h].at[pl.ds(OWN, OWN)], s_p.at[h], r_p.at[h], partner
+        ).start()
+
+    def stage_b(r, h):
+        last = r + 1 == ROUNDS
+        await_bytes(ratio[h].at[pl.ds(OWN, OWN)], r_p.at[h])
+        backproject(h)
+        if r > 0:
+            await_bytes(rest.at[r - 1, h], r_l.at[r - 1, h])
+            if not last:
+                await_bytes(send_high.at[h], s_h.at[r - 1, h])
+                await_bytes(send_low.at[h], s_l.at[r - 1, h])
+        for v in range(VOX):
+            if r == 0:
+                held = images[frames(h), v * B : (v + 1) * B]
+            else:
+                held = low[r][h][v].astype(f32) + rest[r - 1, h, v].astype(f32)
+            held = held * acc_back[table[LAST_V + v]] * inverse[v]
+            if last:
+                out[frames(h), v * B : (v + 1) * B] = held
+            else:
+                high = held.astype(bf16)
+                send_high[h, v] = high
+                send_low[h, v] = (held - high.astype(f32)).astype(bf16)
+        if not last:
+            remote(send_high.at[h], low[r + 1][h], s_h.at[r, h], r_h.at[r, h], ahead).start()
+            remote(send_low.at[h], rest.at[r, h], s_l.at[r, h], r_l.at[r, h], ahead).start()
+
+    def sensitivity():
+        ones = jnp.ones((F, B), bf16)
+        for t in range(SLOTS):
+            column = jnp.dot(ones, tiles[0, t], preferred_element_type=f32)
+            acc_back[t] = column + acc_back[table[PREV_V + t]]
+        for v in range(VOX):
+            inverse[v] = 1.0 / acc_back[table[LAST_V + v]]
+
     for r in range(ROUNDS):
-        p = r % 2
-        last = r + 1 == ROUNDS
-        for h in range(HALVES):
-            if r > 0:
-                await_bytes(low[r][h], r_h.at[r - 1, h])
-                await_bytes(send_c.at[h], s_c.at[h])
-            project(r, h)
-            if r == 0 and h == 0:
-                pl.semaphore_wait(barrier, len(everyone))
-                for k in far_first_z:
-                    remote(cnt.at[z], cnt.at[z], s_n, r_n, z_peers[k]).start()
-            remote(send_c.at[h], recv_c.at[h], s_c.at[h], r_c.at[h], partner).start()
-        for h in range(HALVES):
-            await_bytes(recv_c.at[h], r_c.at[h])
-            if r > 0:
-                await_bytes(recv_y.at[h], s_y.at[h])
-                await_bytes(ratio[h].at[pl.ds(0, OWN)], s_p.at[h])
-            for j in range(OWN):
-                own = acc[h][table[LAST_R + 2 * j + core]]
-                send_y[h, j] = (own + recv_c[h, j].astype(f32)).astype(bf16)
-            for k in far_first_y:
-                remote(
-                    send_y.at[h, pl.ds(y_of[k] * NZ, NZ)], recv_y.at[h, k - 1],
-                    s_y.at[h], r_y.at[h], y_peers[k],
-                ).start()
+        stage_c(r, 0)
+        if r > 0:
+            stage_b(r - 1, 1)
+        stage_y(r, 0)
+        stage_c(r, 1)
+        stage_y(r, 1)
         if r == 0:
-            ones = jnp.ones((F, B), bf16)
-            for t in range(SLOTS):
-                column = jnp.dot(ones, tiles[0, t], preferred_element_type=f32)
-                acc_back[t] = column + acc_back[table[PREV_V + t]]
-            for v in range(VOX):
-                inverse[v] = 1.0 / acc_back[table[LAST_V + v]]
+            for k in far_first_z:
+                remote(cnt.at[z], cnt.at[z], s_n, r_n, z_peers[k]).start()
+            sensitivity()
+        stage_z(r, 0)
+        stage_z(r, 1)
+        if r == 0:
             await_bytes(cnt.at[pl.ds(0, NZ - 1)], r_n)
-        for h in range(HALVES):
-            await_bytes(recv_y.at[h], r_y.at[h])
-            if r > 1:
-                await_bytes(recv_z.at[p, h], s_z.at[p, h])
-            for b in range(NZ):
-                total = send_y[h, y * NZ + b].astype(f32)
-                for k in range(NY - 1):
-                    total = total + recv_y[h, k, b].astype(f32)
-                send_z[p, h, b] = total.astype(bf16)
-            for k in far_first_z:
-                remote(
-                    send_z.at[p, h], recv_z.at[p, h, k - 1], s_z.at[p, h], r_z.at[p, h], z_peers[k]
-                ).start()
-        for h in range(HALVES):
-            await_bytes(recv_z.at[p, h], r_z.at[p, h])
-            if r > 0:
-                await_bytes(ratio[h].at[pl.ds(0, NZ * (NY - 1))], s_g.at[h])
-            for b in range(NZ):
-                even = send_z[p, h, b].astype(f32) + recv_z[p, h, 1, b].astype(f32)
-                odd = recv_z[p, h, 0, b].astype(f32) + recv_z[p, h, 2, b].astype(f32)
-                measured = cnt[b, r, frames(h), :].astype(f32)
-                ratio[h][y * NZ + b] = (measured / (even + odd)).astype(bf16)
-            mine = ratio[h].at[pl.ds(y * NZ, NZ)]
-            for k in far_first_y:
-                remote(mine, mine, s_g.at[h], r_g.at[h], y_peers[k]).start()
-        for h in range(HALVES):
-            await_bytes(ratio[h].at[pl.ds(0, NZ * (NY - 1))], r_g.at[h])
-            remote(
-                ratio[h].at[pl.ds(0, OWN)], ratio[h].at[pl.ds(OWN, OWN)], s_p.at[h], r_p.at[h], partner
-            ).start()
-        for h in range(HALVES):
-            await_bytes(ratio[h].at[pl.ds(OWN, OWN)], r_p.at[h])
-            backproject(h)
-            if r > 0:
-                await_bytes(rest.at[r - 1, h], r_l.at[r - 1, h])
-                if not last:
-                    await_bytes(send_high.at[h], s_h.at[r - 1, h])
-                    await_bytes(send_low.at[h], s_l.at[r - 1, h])
-            for v in range(VOX):
-                if r == 0:
-                    held = images[frames(h), v * B : (v + 1) * B]
-                else:
-                    held = low[r][h][v].astype(f32) + rest[r - 1, h, v].astype(f32)
-                held = held * acc_back[table[LAST_V + v]] * inverse[v]
-                if last:
-                    out[frames(h), v * B : (v + 1) * B] = held
-                else:
-                    high = held.astype(bf16)
-                    send_high[h, v] = high
-                    send_low[h, v] = (held - high.astype(f32)).astype(bf16)
-            if not last:
-                remote(send_high.at[h], low[r + 1][h], s_h.at[r, h], r_h.at[r, h], ahead).start()
-                remote(send_low.at[h], rest.at[r, h], s_l.at[r, h], r_l.at[r, h], ahead).start()
+        stage_g(r, 0)
+        stage_g(r, 1)
+        stage_p(0)
+        stage_b(r, 0)
+        stage_p(1)
+    stage_b(ROUNDS - 1, 1)
 
     await_bytes(cnt.at[pl.ds(0, NZ - 1)], s_n)
     for h in range(HALVES):

time: 120 us -> 114 us (0.950)
  Pallas kernels: 118 us -> 111 us
    pallas_call x1, Pallas kernels: 116 us -> 109 us  [shards(): pl.pallas_call(fused, out_shape=jax.ShapeDtypeStruct(images.shape, f32),...]
where the time goes in v2:
time: 114 us; the launch traced here: 113 us
  Pallas kernels  111 us (97%)
  local copies, waits for them, and re-layouts  1.67 us (1%)
    pallas_call x1, Pallas kernels, shards(): pl.pallas_call(fused, out_shape=jax.ShapeDtypeStruct(images.shape, f32),...  109 us

profile of v2, /device:TPU:1, one launch (start us, length us, event | category | flops | bytes accessed | tf_op | source)
XLA Modules:
  0.0 113.4 jit_solution(7103860716021500721)
XLA Ops:
  0.7 1.7 %prepare.1.table = s32[256]{0:T(256)} custom-call(s32[1,32]{1,0:T(1,128)} %vox_ref.1, s32[1,32]{1,0:T(1,128)} %ray_ref.1, s32[1,1]{1,0:T(1,128)S(6)} %copy.8.live_ref), custom_call_target="tpu_custom_call" | custom-call | tf_op jit(solution)/shard_map/prepare/pallas_call | solution.py:246
  2.3 109.4 %fused.1 = f32[32,2048]{1,0:T(8,128)} custom-call(s32[256]{0:T(256)} %prepare.1.table, f32[32,2048]{1,0:T(8,128)} %images.1, bf16[1,32,128,128]{3,2,1,0:T(8,128)(2,1)} %tiles.1, s32[1,256,128]{2,1,0:T(8,128)} %counts.1), custom_call_target="tpu_custom_call" | custom-call | tf_op jit(solution)/shard_map/fused/pallas_call | solution.py:255
  111.7 1.7 %copy.9 = f32[32,2048]{1,0:T(8,128)} copy(f32[32,2048]{1,0:T(8,128)} %fused.1) | data formatting | bytes 524288

commit v3 on v2

--- a/solution.py
+++ b/solution.py
@@ -20,35 +20,22 @@
 HALVES = 2
 F = FP // HALVES
 OWN = RAYS // 2
-
-PREV_R, PREV_V, VOX_OF, RATIO_OF, LAST_R, LAST_V, TABLE = 0, 32, 64, 96, 128, 192, 256
+PARTS = 4
+
+PREV_R, PREV_V, LAST_R, LAST_V, TABLE = 0, 1, 2, 3, 8
 
 f32 = jnp.float32
 bf16 = jnp.bfloat16
 
 
-def prepare(vox_ref, ray_ref, live_ref, table_ref):
-    core = lax.rem(lax.axis_index("tile"), 2)
-    live = live_ref[0, 0]
-    for i in range(TABLE):
-        table_ref[i] = SLOTS
-    for t in range(SLOTS):
-        vox, ray = vox_ref[0, t], ray_ref[0, t]
-        table_ref[VOX_OF + t] = vox
-        table_ref[RATIO_OF + t] = jnp.where(lax.rem(ray, 2) == core, 0, OWN) + lax.div(ray, 2)
-        alive = t // TILE_GROUP < live
-        for last, prev, block in ((LAST_R, PREV_R, ray), (LAST_V, PREV_V, vox)):
-            before = table_ref[last + block]
-            table_ref[prev + t] = before
-            table_ref[last + block] = jnp.where(alive, t, before)
-
-
 def fused(
-    table, images, tiles, counts, out,
+    vox_of, ray_of, live, vox_row, ray_row, images_hbm, tiles_hbm, counts_hbm, out_hbm,
+    images, tiles, counts, out, table_rows, table,
     low_0a, low_0b, low_1a, low_1b, low_2a, low_2b, low_3a, low_3b,
     rest, send_high, send_low, acc_a, acc_b, acc_back, inverse,
     send_c, recv_c, send_y, recv_y, send_z, recv_z, ratio_a, ratio_b, cnt,
     s_c, r_c, s_y, r_y, s_z, r_z, s_g, r_g, s_p, r_p, s_h, r_h, s_l, r_l, s_n, r_n,
+    s_images, s_tiles, s_counts, s_table, s_out,
 ):
     low = ((low_0a, low_0b), (low_1a, low_1b), (low_2a, low_2b), (low_3a, low_3b))
     acc = (acc_a, acc_b)
@@ -88,32 +75,67 @@
     def frames(h):
         return slice(h * F, (h + 1) * F)
 
-    for h in range(HALVES):
-        acc[h][SLOTS] = jnp.zeros((F, B), f32)
-        for v in range(VOX):
-            low[0][h][v] = images[frames(h), v * B : (v + 1) * B].astype(bf16)
-    acc_back[SLOTS] = jnp.zeros((F, B), f32)
+    copies = [pltpu.make_async_copy(images_hbm, images, s_images)]
+    for i in range(PARTS):
+        part = pl.ds(i * SLOTS // PARTS, SLOTS // PARTS)
+        copies.append(pltpu.make_async_copy(tiles_hbm.at[0, part], tiles.at[part], s_tiles.at[i]))
     for r in range(ROUNDS):
         panel = lax.rem(subset - r + SUBSETS, SUBSETS)
         rows = pl.ds(pl.multiple_of(panel * FP, FP), FP)
-        cnt[z, r] = counts[0, rows, :].astype(f32).astype(bf16)
+        copies.append(pltpu.make_async_copy(counts_hbm.at[0, rows], counts.at[r], s_counts.at[r]))
+    for copy in copies:
+        copy.start()
+
+    slot = lax.broadcasted_iota(jnp.int32, (SLOTS, SLOTS), 0)
+    later = lax.broadcasted_iota(jnp.int32, (SLOTS, SLOTS), 1)
+
+    def latest(found):
+        best = jnp.max(jnp.where(found, lax.broadcasted_iota(jnp.int32, found.shape, 0), -1), axis=0, keepdims=True)
+        return jnp.where(best < 0, SLOTS, best)
+
+    for block_of, row, prev, last, blocks in (
+        (ray_of, ray_row, PREV_R, LAST_R, RAYS),
+        (vox_of, vox_row, PREV_V, LAST_V, VOX),
+    ):
+        column = jnp.zeros((SLOTS, B), jnp.int32)
+        which = lax.broadcasted_iota(jnp.int32, (SLOTS, B), 0)
+        for t in range(SLOTS):
+            column = jnp.where(which == t, block_of[0, t], column)
+        column = jnp.where(which // TILE_GROUP < live[0, 0], column, -1)
+        same = column[:, :SLOTS] == jnp.broadcast_to(row[...], (SLOTS, SLOTS))
+        table_rows[prev : prev + 1, :SLOTS] = latest(same & (slot < later))
+        block = lax.broadcasted_iota(jnp.int32, (SLOTS, B), 1)
+        table_rows[last : last + 1, :] = latest(column == block)
+    table_copy = pltpu.make_async_copy(table_rows, table, s_table)
+    table_copy.start()
+
+    for h in range(HALVES):
+        acc[h][SLOTS] = jnp.zeros((F, B), f32)
+    acc_back[SLOTS] = jnp.zeros((F, B), f32)
+    copies[0].wait()
+    for h in range(HALVES):
+        for v in range(VOX):
+            low[0][h][v] = images[frames(h), v * B : (v + 1) * B].astype(bf16)
+    table_copy.wait()
 
     def project(r, h):
         for t in range(SLOTS):
-            chosen = low[r][h][table[VOX_OF + t]]
+            if r == 0 and h == 0 and t % (SLOTS // PARTS) == 0:
+                copies[1 + t // (SLOTS // PARTS)].wait()
+            chosen = low[r][h][vox_of[0, t]]
             product = lax.dot_general(
-                chosen, tiles[0, t], (((1,), (1,)), ((), ())), preferred_element_type=f32
+                chosen, tiles[t], (((1,), (1,)), ((), ())), preferred_element_type=f32
             )
-            acc[h][t] = product + acc[h][table[PREV_R + t]]
+            acc[h][t] = product + acc[h][table[PREV_R, t]]
         for j in range(OWN):
-            send_c[h, j] = acc[h][table[LAST_R + 2 * j + 1 - core]].astype(bf16)
+            send_c[h, j] = acc[h][table[LAST_R, 2 * j + 1 - core]].astype(bf16)
 
     def backproject(h):
         for t in range(SLOTS):
-            product = jnp.dot(
-                ratio[h][table[RATIO_OF + t]], tiles[0, t], preferred_element_type=f32
-            )
-            acc_back[t] = product + acc_back[table[PREV_V + t]]
+            ray = ray_of[0, t]
+            place = jnp.where(lax.rem(ray, 2) == core, 0, OWN) + lax.div(ray, 2)
+            product = jnp.dot(ratio[h][place], tiles[t], preferred_element_type=f32)
+            acc_back[t] = product + acc_back[table[PREV_V, t]]
 
     def stage_c(r, h):
         if r > 0:
@@ -130,7 +152,7 @@
             await_bytes(recv_y.at[h], s_y.at[h])
             await_bytes(ratio[h].at[pl.ds(0, OWN)], s_p.at[h])
         for j in range(OWN):
-            own = acc[h][table[LAST_R + 2 * j + core]]
+            own = acc[h][table[LAST_R, 2 * j + core]]
             send_y[h, j] = (own + recv_c[h, j].astype(f32)).astype(bf16)
         for k in far_first_y:
             remote(
@@ -187,33 +209,36 @@
                 held = images[frames(h), v * B : (v + 1) * B]
             else:
                 held = low[r][h][v].astype(f32) + rest[r - 1, h, v].astype(f32)
-            held = held * acc_back[table[LAST_V + v]] * inverse[v]
+            held = held * acc_back[table[LAST_V, v]] * inverse[v]
             if last:
                 out[frames(h), v * B : (v + 1) * B] = held
             else:
                 high = held.astype(bf16)
                 send_high[h, v] = high
                 send_low[h, v] = (held - high.astype(f32)).astype(bf16)
-        if not last:
+        if last:
+            pltpu.make_async_copy(out.at[frames(h)], out_hbm.at[frames(h)], s_out.at[h]).start()
+        else:
             remote(send_high.at[h], low[r + 1][h], s_h.at[r, h], r_h.at[r, h], ahead).start()
             remote(send_low.at[h], rest.at[r, h], s_l.at[r, h], r_l.at[r, h], ahead).start()
 
     def sensitivity():
         ones = jnp.ones((F, B), bf16)
         for t in range(SLOTS):
-            column = jnp.dot(ones, tiles[0, t], preferred_element_type=f32)
-            acc_back[t] = column + acc_back[table[PREV_V + t]]
+            column = jnp.dot(ones, tiles[t], preferred_element_type=f32)
+            acc_back[t] = column + acc_back[table[PREV_V, t]]
         for v in range(VOX):
-            inverse[v] = 1.0 / acc_back[table[LAST_V + v]]
+            inverse[v] = 1.0 / acc_back[table[LAST_V, v]]
 
     for r in range(ROUNDS):
         stage_c(r, 0)
-        if r > 0:
-            stage_b(r - 1, 1)
         stage_y(r, 0)
         stage_c(r, 1)
         stage_y(r, 1)
         if r == 0:
+            for i in range(ROUNDS):
+                copies[1 + PARTS + i].wait()
+                cnt[z, i] = counts[i].astype(f32).astype(bf16)
             for k in far_first_z:
                 remote(cnt.at[z], cnt.at[z], s_n, r_n, z_peers[k]).start()
             sensitivity()
@@ -226,7 +251,7 @@
         stage_p(0)
         stage_b(r, 0)
         stage_p(1)
-    stage_b(ROUNDS - 1, 1)
+        stage_b(r, 1)
 
     await_bytes(cnt.at[pl.ds(0, NZ - 1)], s_n)
     for h in range(HALVES):
@@ -238,26 +263,29 @@
         await_bytes(ratio[h].at[pl.ds(0, OWN)], s_p.at[h])
         await_bytes(send_high.at[h], s_h.at[ROUNDS - 2, h])
         await_bytes(send_low.at[h], s_l.at[ROUNDS - 2, h])
+        pltpu.make_async_copy(out.at[frames(h)], out_hbm.at[frames(h)], s_out.at[h]).wait()
 
 
 def shards(images, system_tiles, tile_vox, tile_ray, live_blocks, counts):
     smem = pl.BlockSpec(memory_space=pltpu.SMEM)
     vmem = pl.BlockSpec(memory_space=pltpu.VMEM)
-    table = pl.pallas_call(
-        prepare,
-        out_shape=jax.ShapeDtypeStruct((TABLE,), jnp.int32),
-        in_specs=[smem] * 3,
-        out_specs=smem,
-        name="prepare",
-    )(tile_vox, tile_ray, live_blocks)
+    hbm = pl.BlockSpec(memory_space=pl.ANY)
     half = pltpu.VMEM((VOX, F, B), bf16)
     dma = pltpu.SemaphoreType.DMA
     return pl.pallas_call(
         fused,
         out_shape=jax.ShapeDtypeStruct(images.shape, f32),
-        in_specs=[smem, vmem, vmem, vmem],
-        out_specs=vmem,
-        scratch_shapes=[half] * (2 * ROUNDS)
+        in_specs=[smem, smem, smem, vmem, vmem, hbm, hbm, hbm],
+        out_specs=hbm,
+        scratch_shapes=[
+            pltpu.VMEM((FP, VOX * B), f32),
+            pltpu.VMEM((SLOTS, B, B), bf16),
+            pltpu.VMEM((ROUNDS, FP, B), jnp.int32),
+            pltpu.VMEM((FP, VOX * B), f32),
+            pltpu.VMEM((TABLE, B), jnp.int32),
+            pltpu.SMEM((TABLE, B), jnp.int32),
+        ]
+        + [half] * (2 * ROUNDS)
         + [
             pltpu.VMEM((ROUNDS - 1, HALVES, VOX, F, B), bf16),
             pltpu.VMEM((HALVES, VOX, F, B), bf16),
@@ -283,10 +311,11 @@
             dma((ROUNDS - 1, HALVES)), dma((ROUNDS - 1, HALVES)),
             dma((ROUNDS - 1, HALVES)), dma((ROUNDS - 1, HALVES)),
             dma, dma,
+            dma, dma((PARTS,)), dma((ROUNDS,)), dma, dma((HALVES,)),
         ],
         compiler_params=pltpu.CompilerParams(collective_id=0, has_side_effects=True),
         name="fused",
-    )(table, images, system_tiles, counts)
+    )(tile_vox, tile_ray, live_blocks, tile_vox, tile_ray, images, system_tiles, counts)
 
 
 def solution(mesh):

time: 114 us -> 109 us (0.956)
  Pallas kernels: 111 us -> 106 us
    pallas_call x1, Pallas kernels: 109 us -> 106 us  [shards(): pl.pallas_call(fused, out_shape=jax.ShapeDtypeStruct(images.shape, f32),...]
    pallas_call x1 -> x0, Pallas kernels: 1.68 us -> none  [shards(): pl.pallas_call(prepare, out_shape=jax.ShapeDtypeStruct((TABLE,), jnp.int3...]
where the time goes in v3:
time: 109 us
  Pallas kernels  106 us (97%)
  local copies, waits for them, and re-layouts  1.67 us (2%)
    pallas_call x1, Pallas kernels, shards(): pl.pallas_call(fused, out_shape=jax.ShapeDtypeStruct(images.shape, f32),...  106 us

profile of v3, /device:TPU:1, one launch (start us, length us, event | category | flops | bytes accessed | tf_op | source)
XLA Modules:
  0.0 108.6 jit_solution(2313103534743289116)
XLA Ops:
  0.7 106.3 %fused.1 = f32[32,2048]{1,0:T(8,128)} custom-call(s32[1,32]{1,0:T(1,128)} %vox_row.1, s32[1,32]{1,0:T(1,128)} %ray_row.1, s32[1,1]{1,0:T(1,128)S(6)} %copy.8.live, s32[1,32]{1,0:T(1,128)} %vox_row.1, s32[1,32]{1,0:T(1,128)} %ray_row.1, f32[32,2048]{1,0:T(8,128)} %images_hbm.1, bf16[1,32,128,128]{3,2,1,0:T(8,128)(2,1)} %tiles_hbm.1, s32[1,256,128]{2,1,0:T(8,128)} %counts_hbm.1), custom_call_target="tpu_custom_call" | custom-call | tf_op jit(solution)/shard_map/fused/pallas_call | solution.py:275
  106.9 1.7 %copy.9 = f32[32,2048]{1,0:T(8,128)} copy(f32[32,2048]{1,0:T(8,128)} %fused.1) | data formatting | bytes 524288

commit v4 on v3

--- a/solution.py
+++ b/solution.py
@@ -21,21 +21,26 @@
 F = FP // HALVES
 OWN = RAYS // 2
 PARTS = 4
-
-PREV_R, PREV_V, LAST_R, LAST_V, TABLE = 0, 1, 2, 3, 8
+PIECES = 8
+LENT = 2
+OWN_ROUNDS = (0, 1, 3)
+
+PREV_R, PREV_V, LAST_R, LAST_V, PLACE, VOX_OF, TABLE = 0, 1, 2, 3, 4, 5, 8
 
 f32 = jnp.float32
 bf16 = jnp.bfloat16
 
 
 def fused(
-    vox_of, ray_of, live, vox_row, ray_row, images_hbm, tiles_hbm, counts_hbm, out_hbm,
-    images, tiles, counts, out, table_rows, table,
+    images_hbm, tiles_hbm, vox_hbm, ray_hbm, live_hbm, counts_hbm, out_hbm,
+    vox_of, ray_of, live, vox_row, ray_row, images, own_tiles, counts, out, table_rows, own_table,
+    lent_tiles, lent_rows, lent_table, lent_inverse, count_out, count_in, lent_cnt,
     low_0a, low_0b, low_1a, low_1b, low_2a, low_2b, low_3a, low_3b,
-    rest, send_high, send_low, acc_a, acc_b, acc_back, inverse,
+    rest, send_high, send_low, acc_a, acc_b, acc_back, own_inverse,
     send_c, recv_c, send_y, recv_y, send_z, recv_z, ratio_a, ratio_b, cnt,
     s_c, r_c, s_y, r_y, s_z, r_z, s_g, r_g, s_p, r_p, s_h, r_h, s_l, r_l, s_n, r_n,
-    s_images, s_tiles, s_counts, s_table, s_out,
+    s_index, s_images, s_tiles, s_counts, s_table, s_out,
+    s_t, r_t, s_i, r_i, s_k, r_k, s_m, r_m,
 ):
     low = ((low_0a, low_0b), (low_1a, low_1b), (low_2a, low_2b), (low_3a, low_3b))
     acc = (acc_a, acc_b)
@@ -55,7 +60,9 @@
     z_peers = [None] + [at(y, lax.rem(z + k, NZ), core) for k in range(1, NZ)]
     ahead = {"subset": lax.rem(subset + 1, SUBSETS)}
     behind = {"subset": lax.rem(subset + SUBSETS - 1, SUBSETS)}
-    everyone = [partner] + y_peers[1:] + z_peers[1:] + [ahead, behind]
+    ahead_two = {"subset": lax.rem(subset + 2, SUBSETS)}
+    behind_two = {"subset": lax.rem(subset + SUBSETS - 2, SUBSETS)}
+    everyone = [partner] + y_peers[1:] + z_peers[1:] + [ahead, behind, ahead_two, behind_two]
     far_first_y = (4, 3, 5, 2, 6, 1, 7)
     far_first_z = (2, 1, 3)
 
@@ -75,16 +82,26 @@
     def frames(h):
         return slice(h * F, (h + 1) * F)
 
+    indices = [
+        pltpu.make_async_copy(src, dst, s_index.at[i])
+        for i, (src, dst) in enumerate(
+            ((vox_hbm, vox_of), (ray_hbm, ray_of), (live_hbm, live), (vox_hbm, vox_row), (ray_hbm, ray_row))
+        )
+    ]
+    for copy in indices:
+        copy.start()
     copies = [pltpu.make_async_copy(images_hbm, images, s_images)]
     for i in range(PARTS):
         part = pl.ds(i * SLOTS // PARTS, SLOTS // PARTS)
-        copies.append(pltpu.make_async_copy(tiles_hbm.at[0, part], tiles.at[part], s_tiles.at[i]))
+        copies.append(pltpu.make_async_copy(tiles_hbm.at[0, part], own_tiles.at[part], s_tiles.at[i]))
     for r in range(ROUNDS):
         panel = lax.rem(subset - r + SUBSETS, SUBSETS)
         rows = pl.ds(pl.multiple_of(panel * FP, FP), FP)
         copies.append(pltpu.make_async_copy(counts_hbm.at[0, rows], counts.at[r], s_counts.at[r]))
     for copy in copies:
         copy.start()
+    for copy in indices:
+        copy.wait()
 
     slot = lax.broadcasted_iota(jnp.int32, (SLOTS, SLOTS), 0)
     later = lax.broadcasted_iota(jnp.int32, (SLOTS, SLOTS), 1)
@@ -106,7 +123,11 @@
         table_rows[prev : prev + 1, :SLOTS] = latest(same & (slot < later))
         block = lax.broadcasted_iota(jnp.int32, (SLOTS, B), 1)
         table_rows[last : last + 1, :] = latest(column == block)
-    table_copy = pltpu.make_async_copy(table_rows, table, s_table)
+    ray = ray_row[...]
+    place = jnp.where(ray % 2 == core, 0, OWN) + ray // 2
+    table_rows[PLACE : PLACE + 1, :SLOTS] = place
+    table_rows[VOX_OF : VOX_OF + 1, :SLOTS] = vox_row[...]
+    table_copy = pltpu.make_async_copy(table_rows, own_table, s_table.at[0])
     table_copy.start()
 
     for h in range(HALVES):
@@ -118,28 +139,39 @@
             low[0][h][v] = images[frames(h), v * B : (v + 1) * B].astype(bf16)
     table_copy.wait()
 
+    def with_tiles(r):
+        return (lent_tiles, lent_table, lent_inverse) if r == LENT else (own_tiles, own_table, own_inverse)
+
     def project(r, h):
-        for t in range(SLOTS):
+        tiles, table, _ = with_tiles(r)
+        for t in range(0, SLOTS, 2):
             if r == 0 and h == 0 and t % (SLOTS // PARTS) == 0:
                 copies[1 + t // (SLOTS // PARTS)].wait()
-            chosen = low[r][h][vox_of[0, t]]
+            chosen = jnp.concatenate([low[r][h][table[VOX_OF, t + i]] for i in range(2)], axis=0)
+            pair = tiles[t : t + 2].reshape(2 * B, B)
             product = lax.dot_general(
-                chosen, tiles[t], (((1,), (1,)), ((), ())), preferred_element_type=f32
+                chosen, pair, (((1,), (1,)), ((), ())), preferred_element_type=f32
             )
-            acc[h][t] = product + acc[h][table[PREV_R, t]]
+            for i in range(2):
+                mine = product[i * F : (i + 1) * F, i * B : (i + 1) * B]
+                acc[h][t + i] = mine + acc[h][table[PREV_R, t + i]]
         for j in range(OWN):
             send_c[h, j] = acc[h][table[LAST_R, 2 * j + 1 - core]].astype(bf16)
 
-    def backproject(h):
-        for t in range(SLOTS):
-            ray = ray_of[0, t]
-            place = jnp.where(lax.rem(ray, 2) == core, 0, OWN) + lax.div(ray, 2)
-            product = jnp.dot(ratio[h][place], tiles[t], preferred_element_type=f32)
-            acc_back[t] = product + acc_back[table[PREV_V, t]]
+    def backproject(r, h):
+        tiles, table, _ = with_tiles(r)
+        for t in range(0, SLOTS, 2):
+            chosen = jnp.concatenate([ratio[h][table[PLACE, t + i]] for i in range(2)], axis=0)
+            pair = jnp.concatenate([tiles[t], tiles[t + 1]], axis=1)
+            product = jnp.dot(chosen, pair, preferred_element_type=f32)
+            for i in range(2):
+                mine = product[i * F : (i + 1) * F, i * B : (i + 1) * B]
+                acc_back[t + i] = mine + acc_back[table[PREV_V, t + i]]
 
     def stage_c(r, h):
+        if 0 < r <= LENT:
+            await_bytes(low[r][h], r_h.at[r - 1, h])
         if r > 0:
-            await_bytes(low[r][h], r_h.at[r - 1, h])
             await_bytes(send_c.at[h], s_c.at[h])
         project(r, h)
         if r == 0 and h == 0:
@@ -147,6 +179,7 @@
         remote(send_c.at[h], recv_c.at[h], s_c.at[h], r_c.at[h], partner).start()
 
     def stage_y(r, h):
+        table = with_tiles(r)[1]
         await_bytes(recv_c.at[h], r_c.at[h])
         if r > 0:
             await_bytes(recv_y.at[h], s_y.at[h])
@@ -183,7 +216,10 @@
         for b in range(NZ):
             even = send_z[p, h, b].astype(f32) + recv_z[p, h, 1, b].astype(f32)
             odd = recv_z[p, h, 0, b].astype(f32) + recv_z[p, h, 2, b].astype(f32)
-            measured = cnt[b, r, frames(h), :].astype(f32)
+            if r == LENT:
+                measured = lent_cnt[b, frames(h), :].astype(f32)
+            else:
+                measured = cnt[b, OWN_ROUNDS.index(r), frames(h), :].astype(f32)
             ratio[h][y * NZ + b] = (measured / (even + odd)).astype(bf16)
         mine = ratio[h].at[pl.ds(y * NZ, NZ)]
         for k in far_first_y:
@@ -197,32 +233,39 @@
 
     def stage_b(r, h):
         last = r + 1 == ROUNDS
+        _, table, inverse = with_tiles(r)
         await_bytes(ratio[h].at[pl.ds(OWN, OWN)], r_p.at[h])
-        backproject(h)
-        if r > 0:
+        backproject(r, h)
+        if 0 < r <= LENT:
             await_bytes(rest.at[r - 1, h], r_l.at[r - 1, h])
-            if not last:
-                await_bytes(send_high.at[h], s_h.at[r - 1, h])
-                await_bytes(send_low.at[h], s_l.at[r - 1, h])
+        if r == 1:
+            await_bytes(send_high.at[h], s_h.at[r - 1, h])
+            await_bytes(send_low.at[h], s_l.at[r - 1, h])
         for v in range(VOX):
             if r == 0:
                 held = images[frames(h), v * B : (v + 1) * B]
+            elif r <= LENT:
+                held = low[r][h][v].astype(f32) + rest[r - 1, h, v].astype(f32)
             else:
-                held = low[r][h][v].astype(f32) + rest[r - 1, h, v].astype(f32)
+                held = out[frames(h), v * B : (v + 1) * B]
             held = held * acc_back[table[LAST_V, v]] * inverse[v]
-            if last:
+            if r >= LENT:
                 out[frames(h), v * B : (v + 1) * B] = held
+                if not last:
+                    low[r + 1][h][v] = held.astype(bf16)
             else:
                 high = held.astype(bf16)
                 send_high[h, v] = high
                 send_low[h, v] = (held - high.astype(f32)).astype(bf16)
         if last:
             pltpu.make_async_copy(out.at[frames(h)], out_hbm.at[frames(h)], s_out.at[h]).start()
-        else:
-            remote(send_high.at[h], low[r + 1][h], s_h.at[r, h], r_h.at[r, h], ahead).start()
-            remote(send_low.at[h], rest.at[r, h], s_l.at[r, h], r_l.at[r, h], ahead).start()
-
-    def sensitivity():
+        elif r < LENT:
+            target = ahead if r == 0 else ahead_two
+            remote(send_high.at[h], low[r + 1][h], s_h.at[r, h], r_h.at[r, h], target).start()
+            remote(send_low.at[h], rest.at[r, h], s_l.at[r, h], r_l.at[r, h], target).start()
+
+    def sensitivity(r):
+        tiles, table, inverse = with_tiles(r)
         ones = jnp.ones((F, B), bf16)
         for t in range(SLOTS):
             column = jnp.dot(ones, tiles[t], preferred_element_type=f32)
@@ -230,29 +273,76 @@
         for v in range(VOX):
             inverse[v] = 1.0 / acc_back[table[LAST_V, v]]
 
+    def lend(i):
+        part = pl.ds(i * SLOTS // PIECES, SLOTS // PIECES)
+        remote(own_tiles.at[part], lent_tiles.at[part], s_t, r_t, ahead).start()
+
+    def share_counts():
+        for k in far_first_z:
+            remote(cnt.at[z], cnt.at[z], s_n, r_n, z_peers[k]).start()
+        remote(count_out, count_in, s_k, r_k, ahead).start()
+        remote(table_rows, lent_rows, s_i, r_i, ahead).start()
+
+    def take_lent():
+        await_bytes(count_in, r_k)
+        lent_cnt[z] = count_in[...]
+        for k in far_first_z:
+            remote(lent_cnt.at[z], lent_cnt.at[z], s_m, r_m, z_peers[k]).start()
+        await_bytes(lent_rows, r_i)
+        lent_copy = pltpu.make_async_copy(lent_rows, lent_table, s_table.at[1])
+        lent_copy.start()
+        lent_copy.wait()
+
+    for i in range(ROUNDS):
+        copies[1 + PARTS + i].wait()
+        measured = counts[i].astype(f32).astype(bf16)
+        if i == LENT:
+            count_out[...] = measured
+        else:
+            cnt[z, OWN_ROUNDS.index(i)] = measured
+
     for r in range(ROUNDS):
         stage_c(r, 0)
+        if r == 0:
+            share_counts()
+        if r == LENT + 1:
+            stage_p(1)
         stage_y(r, 0)
+        if r == LENT + 1:
+            stage_b(LENT, 1)
+        if r < LENT:
+            lend(4 * r)
         stage_c(r, 1)
         stage_y(r, 1)
-        if r == 0:
-            for i in range(ROUNDS):
-                copies[1 + PARTS + i].wait()
-                cnt[z, i] = counts[i].astype(f32).astype(bf16)
-            for k in far_first_z:
-                remote(cnt.at[z], cnt.at[z], s_n, r_n, z_peers[k]).start()
-            sensitivity()
+        if r < LENT:
+            lend(4 * r + 1)
+        if r in (0, LENT):
+            sensitivity(r)
         stage_z(r, 0)
         stage_z(r, 1)
         if r == 0:
             await_bytes(cnt.at[pl.ds(0, NZ - 1)], r_n)
+        if r == LENT:
+            await_bytes(lent_cnt.at[pl.ds(0, NZ - 1)], r_m)
         stage_g(r, 0)
         stage_g(r, 1)
+        if r < LENT:
+            lend(4 * r + 2)
+            lend(4 * r + 3)
+        if r + 1 == LENT:
+            take_lent()
         stage_p(0)
         stage_b(r, 0)
-        stage_p(1)
-        stage_b(r, 1)
-
+        if r != LENT:
+            stage_p(1)
+            stage_b(r, 1)
+        if r + 1 == LENT:
+            await_bytes(lent_tiles, r_t)
+
+    await_bytes(own_tiles, s_t)
+    await_bytes(table_rows, s_i)
+    await_bytes(count_out, s_k)
+    await_bytes(lent_cnt.at[pl.ds(0, NZ - 1)], s_m)
     await_bytes(cnt.at[pl.ds(0, NZ - 1)], s_n)
     for h in range(HALVES):
         await_bytes(send_c.at[h], s_c.at[h])
@@ -261,33 +351,43 @@
             await_bytes(recv_z.at[p, h], s_z.at[p, h])
         await_bytes(ratio[h].at[pl.ds(0, NZ * (NY - 1))], s_g.at[h])
         await_bytes(ratio[h].at[pl.ds(0, OWN)], s_p.at[h])
-        await_bytes(send_high.at[h], s_h.at[ROUNDS - 2, h])
-        await_bytes(send_low.at[h], s_l.at[ROUNDS - 2, h])
+        await_bytes(send_high.at[h], s_h.at[LENT - 1, h])
+        await_bytes(send_low.at[h], s_l.at[LENT - 1, h])
         pltpu.make_async_copy(out.at[frames(h)], out_hbm.at[frames(h)], s_out.at[h]).wait()
 
 
 def shards(images, system_tiles, tile_vox, tile_ray, live_blocks, counts):
-    smem = pl.BlockSpec(memory_space=pltpu.SMEM)
-    vmem = pl.BlockSpec(memory_space=pltpu.VMEM)
     hbm = pl.BlockSpec(memory_space=pl.ANY)
     half = pltpu.VMEM((VOX, F, B), bf16)
     dma = pltpu.SemaphoreType.DMA
     return pl.pallas_call(
         fused,
         out_shape=jax.ShapeDtypeStruct(images.shape, f32),
-        in_specs=[smem, smem, smem, vmem, vmem, hbm, hbm, hbm],
+        in_specs=[hbm] * 6,
         out_specs=hbm,
         scratch_shapes=[
+            pltpu.SMEM((1, SLOTS), jnp.int32),
+            pltpu.SMEM((1, SLOTS), jnp.int32),
+            pltpu.SMEM((1, 1), jnp.int32),
+            pltpu.VMEM((1, SLOTS), jnp.int32),
+            pltpu.VMEM((1, SLOTS), jnp.int32),
             pltpu.VMEM((FP, VOX * B), f32),
             pltpu.VMEM((SLOTS, B, B), bf16),
             pltpu.VMEM((ROUNDS, FP, B), jnp.int32),
             pltpu.VMEM((FP, VOX * B), f32),
             pltpu.VMEM((TABLE, B), jnp.int32),
             pltpu.SMEM((TABLE, B), jnp.int32),
+            pltpu.VMEM((SLOTS, B, B), bf16),
+            pltpu.VMEM((TABLE, B), jnp.int32),
+            pltpu.SMEM((TABLE, B), jnp.int32),
+            pltpu.VMEM((VOX, F, B), f32),
+            pltpu.VMEM((FP, B), bf16),
+            pltpu.VMEM((FP, B), bf16),
+            pltpu.VMEM((NZ, FP, B), bf16),
         ]
         + [half] * (2 * ROUNDS)
         + [
-            pltpu.VMEM((ROUNDS - 1, HALVES, VOX, F, B), bf16),
+            pltpu.VMEM((LENT, HALVES, VOX, F, B), bf16),
             pltpu.VMEM((HALVES, VOX, F, B), bf16),
             pltpu.VMEM((HALVES, VOX, F, B), bf16),
             pltpu.VMEM((SLOTS + 1, F, B), f32),
@@ -302,20 +402,21 @@
             pltpu.VMEM((2, HALVES, NZ - 1, NZ, F, B), bf16),
             pltpu.VMEM((RAYS, F, B), bf16),
             pltpu.VMEM((RAYS, F, B), bf16),
-            pltpu.VMEM((NZ, ROUNDS, FP, B), bf16),
+            pltpu.VMEM((NZ, len(OWN_ROUNDS), FP, B), bf16),
             dma((HALVES,)), dma((HALVES,)),
             dma((HALVES,)), dma((HALVES,)),
             dma((2, HALVES)), dma((2, HALVES)),
             dma((HALVES,)), dma((HALVES,)),
             dma((HALVES,)), dma((HALVES,)),
-            dma((ROUNDS - 1, HALVES)), dma((ROUNDS - 1, HALVES)),
-            dma((ROUNDS - 1, HALVES)), dma((ROUNDS - 1, HALVES)),
+            dma((LENT, HALVES)), dma((LENT, HALVES)),
+            dma((LENT, HALVES)), dma((LENT, HALVES)),
             dma, dma,
-            dma, dma((PARTS,)), dma((ROUNDS,)), dma, dma((HALVES,)),
+            dma((5,)), dma, dma((PARTS,)), dma((ROUNDS,)), dma((2,)), dma((HALVES,)),
+            dma, dma, dma, dma, dma, dma, dma, dma,
         ],
         compiler_params=pltpu.CompilerParams(collective_id=0, has_side_effects=True),
         name="fused",
-    )(tile_vox, tile_ray, live_blocks, tile_vox, tile_ray, images, system_tiles, counts)
+    )(images, system_tiles, tile_vox, tile_ray, live_blocks, counts)
 
 
 def solution(mesh):

time: 109 us -> 106 us (0.972)
  Pallas kernels: 106 us -> 103 us
    pallas_call x1, Pallas kernels: 106 us -> 103 us  [shards(): pl.pallas_call(fused, out_shape=jax.ShapeDtypeStruct(images.shape, f32),...]
where the time goes in v4:
time: 106 us
  Pallas kernels  103 us (97%)
  local copies, waits for them, and re-layouts  1.67 us (2%)
    pallas_call x1, Pallas kernels, shards(): pl.pallas_call(fused, out_shape=jax.ShapeDtypeStruct(images.shape, f32),...  103 us

profile of v4, /device:TPU:1, one launch (start us, length us, event | category | flops | bytes accessed | tf_op | source)
XLA Modules:
  0.0 105.6 jit_solution(7226498960882710604)
XLA Ops:
  0.7 103.3 %fused.1 = f32[32,2048]{1,0:T(8,128)} custom-call(f32[32,2048]{1,0:T(8,128)} %images_hbm.1, bf16[1,32,128,128]{3,2,1,0:T(8,128)(2,1)} %tiles_hbm.1, s32[1,32]{1,0:T(1,128)} %vox_hbm.1, s32[1,32]{1,0:T(1,128)} %ray_hbm.1, s32[1,1]{1,0:T(1,128)S(6)} %copy.8.live_hbm, s32[1,256,128]{2,1,0:T(8,128)} %counts_hbm.1), custom_call_target="tpu_custom_call" | custom-call | tf_op jit(solution)/shard_map/fused/pallas_call | solution.py:363
  103.9 1.7 %copy.9 = f32[32,2048]{1,0:T(8,128)} copy(f32[32,2048]{1,0:T(8,128)} %fused.1) | data formatting | bytes 524288

commit v5 on v4

--- a/solution.py
+++ b/solution.py
@@ -32,14 +32,14 @@
 
 
 def fused(
-    images_hbm, tiles_hbm, vox_hbm, ray_hbm, live_hbm, counts_hbm, out_hbm,
-    vox_of, ray_of, live, vox_row, ray_row, images, own_tiles, counts, out, table_rows, own_table,
+    images_hbm, tiles_hbm, vox_hbm, ray_hbm, live_hbm, counts_hbm, out,
+    vox_of, ray_of, live, vox_row, ray_row, images, own_tiles, counts, table_rows, own_table,
     lent_tiles, lent_rows, lent_table, lent_inverse, count_out, count_in, lent_cnt,
     low_0a, low_0b, low_1a, low_1b, low_2a, low_2b, low_3a, low_3b,
     rest, send_high, send_low, acc_a, acc_b, acc_back, own_inverse,
     send_c, recv_c, send_y, recv_y, send_z, recv_z, ratio_a, ratio_b, cnt,
     s_c, r_c, s_y, r_y, s_z, r_z, s_g, r_g, s_p, r_p, s_h, r_h, s_l, r_l, s_n, r_n,
-    s_index, s_images, s_tiles, s_counts, s_table, s_out,
+    s_index, s_images, s_tiles, s_counts, s_table,
     s_t, r_t, s_i, r_i, s_k, r_k, s_m, r_m,
 ):
     low = ((low_0a, low_0b), (low_1a, low_1b), (low_2a, low_2b), (low_3a, low_3b))
@@ -257,9 +257,7 @@
                 high = held.astype(bf16)
                 send_high[h, v] = high
                 send_low[h, v] = (held - high.astype(f32)).astype(bf16)
-        if last:
-            pltpu.make_async_copy(out.at[frames(h)], out_hbm.at[frames(h)], s_out.at[h]).start()
-        elif r < LENT:
+        if r < LENT:
             target = ahead if r == 0 else ahead_two
             remote(send_high.at[h], low[r + 1][h], s_h.at[r, h], r_h.at[r, h], target).start()
             remote(send_low.at[h], rest.at[r, h], s_l.at[r, h], r_l.at[r, h], target).start()
@@ -353,7 +351,6 @@
         await_bytes(ratio[h].at[pl.ds(0, OWN)], s_p.at[h])
         await_bytes(send_high.at[h], s_h.at[LENT - 1, h])
         await_bytes(send_low.at[h], s_l.at[LENT - 1, h])
-        pltpu.make_async_copy(out.at[frames(h)], out_hbm.at[frames(h)], s_out.at[h]).wait()
 
 
 def shards(images, system_tiles, tile_vox, tile_ray, live_blocks, counts):
@@ -364,7 +361,7 @@
         fused,
         out_shape=jax.ShapeDtypeStruct(images.shape, f32),
         in_specs=[hbm] * 6,
-        out_specs=hbm,
+        out_specs=pl.BlockSpec(memory_space=pltpu.VMEM),
         scratch_shapes=[
             pltpu.SMEM((1, SLOTS), jnp.int32),
             pltpu.SMEM((1, SLOTS), jnp.int32),
@@ -374,7 +371,6 @@
             pltpu.VMEM((FP, VOX * B), f32),
             pltpu.VMEM((SLOTS, B, B), bf16),
             pltpu.VMEM((ROUNDS, FP, B), jnp.int32),
-            pltpu.VMEM((FP, VOX * B), f32),
             pltpu.VMEM((TABLE, B), jnp.int32),
             pltpu.SMEM((TABLE, B), jnp.int32),
             pltpu.VMEM((SLOTS, B, B), bf16),
@@ -411,10 +407,10 @@
             dma((LENT, HALVES)), dma((LENT, HALVES)),
             dma((LENT, HALVES)), dma((LENT, HALVES)),
             dma, dma,
-            dma((5,)), dma, dma((PARTS,)), dma((ROUNDS,)), dma((2,)), dma((HALVES,)),
+            dma((5,)), dma, dma((PARTS,)), dma((ROUNDS,)), dma((2,)),
             dma, dma, dma, dma, dma, dma, dma, dma,
         ],
-        compiler_params=pltpu.CompilerParams(collective_id=0, has_side_effects=True),
+        compiler_params=pltpu.CompilerParams(collective_id=0, has_side_effects=True, vmem_limit_bytes=56000000),
         name="fused",
     )(images, system_tiles, tile_vox, tile_ray, live_blocks, counts)
 

time: 106 us -> 105 us (level)
    pallas_call x1, Pallas kernels: 103 us -> 102 us  [shards(): pl.pallas_call(fused, out_shape=jax.ShapeDtypeStruct(images.shape, f32),...]
where the time goes in v5:
time: 105 us; the launch traced here: 104 us
  Pallas kernels  102 us (97%)
  local copies, waits for them, and re-layouts  1.61 us (2%)
    pallas_call x1, Pallas kernels, shards(): pl.pallas_call(fused, out_shape=jax.ShapeDtypeStruct(images.shape, f32),...  102 us

profile of v5, /device:TPU:1, one launch (start us, length us, event | category | flops | bytes accessed | tf_op | source)
XLA Modules:
  0.0 104.5 jit_solution(8685746184282060016)
XLA Ops:
  0.0 0.0 copy-start.2
  0.0 0.0 copy-start.1
  0.7 0.0 copy-done.2
  0.7 0.0 copy-done.1
  0.7 0.0 copy-start
  0.7 0.9 copy-done
  1.6 102.1 %fused.1 = f32[32,2048]{1,0:T(8,128)S(1)} custom-call(f32[32,2048]{1,0:T(8,128)} %images_hbm.1, bf16[1,32,128,128]{3,2,1,0:T(8,128)(2,1)} %tiles_hbm.1, s32[1,32]{1,0:T(1,128)S(1)} %copy-done.1, s32[1,32]{1,0:T(1,128)S(1)} %copy-done.2, s32[1,1]{1,0:T(1,128)S(6)} %copy.8.live_hbm, s32[1,256,128]{2,1,0:T(8,128)S(1)} %copy-done), custom_call_target="tpu_custom_call" | custom-call | tf_op jit(solution)/shard_map/fused/pallas_call | solution.py:360
  103.8 0.7 copy.9
Async XLA Ops:
  0.0 0.7 copy-start.2
  0.0 0.7 copy-start.1
  0.7 0.9 copy-start

commit v6 on v5

--- a/solution.py
+++ b/solution.py
@@ -272,8 +272,8 @@
             inverse[v] = 1.0 / acc_back[table[LAST_V, v]]
 
     def lend(i):
-        part = pl.ds(i * SLOTS // PIECES, SLOTS // PIECES)
-        remote(own_tiles.at[part], lent_tiles.at[part], s_t, r_t, ahead).start()
+        for t in range(i * SLOTS // PIECES, (i + 1) * SLOTS // PIECES):
+            remote(own_tiles.at[t], lent_tiles.at[t], s_t, r_t, ahead).start()
 
     def share_counts():
         for k in far_first_z:

time: 105 us -> 105 us (level)
  no operation moved by 1% of the time
where the time goes in v6:
time: 105 us
  Pallas kernels  103 us (98%)
  local copies, waits for them, and re-layouts  1.61 us (2%)
    pallas_call x1, Pallas kernels, shards(): pl.pallas_call(fused, out_shape=jax.ShapeDtypeStruct(images.shape, f32),...  103 us

profile of v6, /device:TPU:1, one launch (start us, length us, event | category | flops | bytes accessed | tf_op | source)
XLA Modules:
  0.0 105.2 jit_solution(1076874518072186884)
XLA Ops:
  0.0 0.0 copy-start.2
  0.0 0.0 copy-start.1
  0.7 0.0 copy-done.2
  0.7 0.0 copy-done.1
  0.7 0.0 copy-start
  0.7 0.9 copy-done
  1.6 102.9 %fused.1 = f32[32,2048]{1,0:T(8,128)S(1)} custom-call(f32[32,2048]{1,0:T(8,128)} %images_hbm.1, bf16[1,32,128,128]{3,2,1,0:T(8,128)(2,1)} %tiles_hbm.1, s32[1,32]{1,0:T(1,128)S(1)} %copy-done.1, s32[1,32]{1,0:T(1,128)S(1)} %copy-done.2, s32[1,1]{1,0:T(1,128)S(6)} %copy.8.live_hbm, s32[1,256,128]{2,1,0:T(8,128)S(1)} %copy-done), custom_call_target="tpu_custom_call" | custom-call | tf_op jit(solution)/shard_map/fused/pallas_call | solution.py:360
  104.5 0.7 copy.9
Async XLA Ops:
  0.0 0.7 copy-start.2
  0.0 0.7 copy-start.1
  0.7 0.9 copy-start
